TPU v7x, 32 devices: a whole 2x2x4 slice. The times are simulated.
32 devices in a mesh: rep: 2 (over x), shard: 16 (over z, y, core).
Axes of the slice: x: 2, y: 2, z: 4, core: 2. Of those that a mesh axis runs over, the one named last changes fastest.
Arguments:
- tokens: bfloat16 [2, 32, 64, 1024], P(None, ('rep', 'shard')), may hold values from -6 to 6
- prefix: int32 [2, 32], P(None, ('rep', 'shard')), may hold values from 6 to 32
- qkv_weight: bfloat16 [1024, 3072], P('shard'), may hold values from -0.1875 to 0.1875
- out_weight: bfloat16 [1024, 1024], P('shard'), may hold values from -1 to 1
- in_weight: bfloat16 [1024, 5632], P('shard'), may hold values from -0.1875 to 0.1875
- down_weight: bfloat16 [2816, 1024], P('shard'), may hold values from -0.109375 to 0.109375
- cotangent: bfloat16 [2, 32, 64, 1024], P(None, ('rep', 'shard')), may hold values from -6 to 6
Outputs:
- result: bfloat16 [2, 32, 64, 1024], P(None, ('rep', 'shard'))
- grad_tokens: float32 [2, 32, 64, 1024], P(None, ('rep', 'shard'))
- grad_qkv: float32 [1024, 3072], P('shard')
- grad_out: float32 [1024, 1024], P('shard')
- grad_in: float32 [1024, 5632], P('shard')
- grad_down: float32 [2816, 1024], P('shard')
Inputs may be any that keep to these rules, and one draw needn't show every extreme that they name: Each sequence's prefix length, a tenth to a half of 64.
All inputs are finite; a program needn't handle non-finite values.
Results may differ from a plain program's by a relative error of at most 0.014.
Values may be sent and summed in bfloat16 or wider, within the bound.
No kernel may reach another device: no remote copies, remote signals or barrier semaphores. Data moves between devices by JAX's collectives and lax.ppermute only.
A program may use at most 256 MiB of HBM per device.

v0:
```python
import jax
import jax.numpy as jnp
from jax import lax
from jax.sharding import PartitionSpec as P

H = 16
HD = 64


def norm_rows(values):
    centre = values - jnp.mean(values, axis=-1, keepdims=True)
    inverse = lax.rsqrt(jnp.mean(centre * centre, axis=-1, keepdims=True) + 1e-05)
    return (centre * inverse, inverse)


def norm_back(normed, inverse, upstream):
    return inverse * (
        upstream
        - jnp.mean(upstream, axis=-1, keepdims=True)
        - normed * jnp.mean(upstream * normed, axis=-1, keepdims=True)
    )


def rope_tables(length, head_size):
    position = jnp.arange(length, dtype=jnp.float32)[:, None]
    frequency = 10000.0 ** (-jnp.arange(0, head_size, 2, dtype=jnp.float32) / head_size)
    angles = position * frequency[None, :]
    angles = jnp.concatenate([angles, angles], axis=-1)
    return (jnp.cos(angles)[:, None, :], jnp.sin(angles)[:, None, :])


def rotate(values, cosine, sine):
    half_size = values.shape[-1] // 2
    turned = jnp.concatenate([-values[..., half_size:], values[..., :half_size]], axis=-1)
    return values * cosine + turned * sine


def rotate_back(grads, cosine, sine):
    half_size = grads.shape[-1] // 2
    scaled = grads * sine
    return grads * cosine + jnp.concatenate(
        [scaled[..., half_size:], -scaled[..., :half_size]], axis=-1
    )


def transpose_dot(left, right):
    return lax.dot_general(
        left, right, (((1,), (1,)), ((), ())), preferred_element_type=jnp.float32
    )


def inner_rows(left, right):
    return lax.dot_general(
        left, right, (((0,), (0,)), ((), ())), preferred_element_type=jnp.float32
    )


def masked_scores(query, keys, allowed, scale):
    scores = jnp.einsum("lhe,mhe->hlm", query, keys, preferred_element_type=jnp.float32) * scale
    return jnp.where(allowed[None], scores, -1e30)


def attend(query, keys, values, allowed, scale):
    scores = masked_scores(query, keys, allowed, scale)
    highest = jnp.max(scores, axis=-1, keepdims=True)
    expo = jnp.exp(scores - highest)
    summed = jnp.sum(expo, axis=-1, keepdims=True)
    probs = (expo / summed).astype(jnp.bfloat16)
    output = jnp.einsum("hlm,mhe->lhe", probs, values, preferred_element_type=jnp.float32)
    return (output, highest + jnp.log(summed))


def attend_back(query, keys, values, log_total, grad_out, allowed, scale):
    probs = jnp.exp(masked_scores(query, keys, allowed, scale) - log_total)
    dprob = jnp.einsum("lhe,mhe->hlm", grad_out, values, preferred_element_type=jnp.float32)
    centre = jnp.sum(probs * dprob, axis=-1, keepdims=True)
    dscore = (probs * (dprob - centre)).astype(jnp.bfloat16)
    dquery = jnp.einsum("hlm,mhe->lhe", dscore, keys, preferred_element_type=jnp.float32) * scale
    dkeys = jnp.einsum("hlm,lhe->mhe", dscore, query, preferred_element_type=jnp.float32) * scale
    dvalues = jnp.einsum(
        "hlm,lhe->mhe", probs.astype(jnp.bfloat16), grad_out, preferred_element_type=jnp.float32
    )
    return (dquery, dkeys, dvalues)


def local(tokens, prefix, qkv_weight, out_weight, in_weight, down_weight, cotangent):
    micro = tokens.shape[0]
    length = tokens.shape[2]
    width = tokens.shape[3]
    hidden_units = down_weight.shape[0] * lax.axis_size("shard")
    scale = HD ** (-0.5)
    cosine, sine = rope_tables(length, HD)
    row_pos = lax.broadcasted_iota(jnp.int32, (length, length), 0)
    col_pos = lax.broadcasted_iota(jnp.int32, (length, length), 1)
    full_set = (
        lax.all_gather(qkv_weight, "shard", axis=0, tiled=True),
        lax.all_gather(out_weight, "shard", axis=0, tiled=True),
        lax.all_gather(in_weight, "shard", axis=0, tiled=True),
        lax.all_gather(down_weight, "shard", axis=0, tiled=True),
    )
    outputs = []
    grad_inputs = []
    kept_h1, kept_gqkv, kept_attn, kept_ga, kept_h2, kept_ggu, kept_hid, kept_gm = (
        [],
        [],
        [],
        [],
        [],
        [],
        [],
        [],
    )
    for batch_index in range(micro):
        xrow = tokens[batch_index, 0].astype(jnp.float32)
        normed_one, inverse_one = norm_rows(xrow)
        first_in = normed_one.astype(jnp.bfloat16)
        mixed = jnp.dot(first_in, full_set[0], preferred_element_type=jnp.float32)
        query = rotate(mixed[:, :width].reshape(length, H, HD), cosine, sine).astype(jnp.bfloat16)
        keys = rotate(mixed[:, width : 2 * width].reshape(length, H, HD), cosine, sine).astype(
            jnp.bfloat16
        )
        values = mixed[:, 2 * width :].reshape(length, H, HD).astype(jnp.bfloat16)
        allowed = (col_pos <= row_pos) | (col_pos < prefix[batch_index, 0])
        attended, log_total = attend(query, keys, values, allowed, scale)
        attn_low = attended.reshape(length, width).astype(jnp.bfloat16)
        middle = xrow + jnp.dot(attn_low, full_set[1], preferred_element_type=jnp.float32)
        normed_two, inverse_two = norm_rows(middle)
        second_in = normed_two.astype(jnp.bfloat16)
        gate_up = jnp.dot(second_in, full_set[2], preferred_element_type=jnp.float32)
        up_part = gate_up[:, :hidden_units]
        gate_part = gate_up[:, hidden_units:]
        sigmoid = jax.nn.sigmoid(gate_part)
        hidden = (gate_part * sigmoid * up_part).astype(jnp.bfloat16)
        final = middle + jnp.dot(hidden, full_set[3], preferred_element_type=jnp.float32)
        outputs.append(final.astype(jnp.bfloat16))
        grad_final = cotangent[batch_index, 0].astype(jnp.float32)
        grad_m = grad_final.astype(jnp.bfloat16)
        grad_hidden = transpose_dot(grad_m, full_set[3])
        grad_up = grad_hidden * (gate_part * sigmoid)
        grad_gate = grad_hidden * up_part * (sigmoid * (1.0 + gate_part * (1.0 - sigmoid)))
        grad_gu = jnp.concatenate([grad_up, grad_gate], axis=-1).astype(jnp.bfloat16)
        grad_mid = grad_final + norm_back(
            normed_two, inverse_two, transpose_dot(grad_gu, full_set[2])
        )
        grad_branch = grad_mid.astype(jnp.bfloat16)
        grad_att = transpose_dot(grad_branch, full_set[1]).astype(jnp.bfloat16)
        dquery, dkeys, dvalues = attend_back(
            query, keys, values, log_total, grad_att.reshape(length, H, HD), allowed, scale
        )
        dquery = rotate_back(dquery, cosine, sine).reshape(length, width)
        dkeys = rotate_back(dkeys, cosine, sine).reshape(length, width)
        grad_mixed = jnp.concatenate(
            [dquery, dkeys, dvalues.reshape(length, width)], axis=-1
        ).astype(jnp.bfloat16)
        grad_input = grad_mid + norm_back(
            normed_one, inverse_one, transpose_dot(grad_mixed, full_set[0])
        )
        grad_inputs.append(grad_input)
        kept_h1.append(first_in)
        kept_gqkv.append(grad_mixed)
        kept_attn.append(attn_low)
        kept_ga.append(grad_branch)
        kept_h2.append(second_in)
        kept_ggu.append(grad_gu)
        kept_hid.append(hidden)
        kept_gm.append(grad_m)
    all_h1 = jnp.concatenate(kept_h1, axis=0)
    all_gqkv = jnp.concatenate(kept_gqkv, axis=0)
    all_attn = jnp.concatenate(kept_attn, axis=0)
    all_ga = jnp.concatenate(kept_ga, axis=0)
    all_h2 = jnp.concatenate(kept_h2, axis=0)
    all_ggu = jnp.concatenate(kept_ggu, axis=0)
    all_hid = jnp.concatenate(kept_hid, axis=0)
    all_gm = jnp.concatenate(kept_gm, axis=0)
    part_one = inner_rows(all_h1, all_gqkv)
    part_two = inner_rows(all_attn, all_ga)
    part_three = inner_rows(all_h2, all_ggu)
    row_share = lax.psum_scatter(
        jnp.concatenate([part_one, part_two, part_three], axis=1),
        "shard",
        scatter_dimension=0,
        tiled=True,
    )
    down_share = lax.psum_scatter(
        inner_rows(all_hid, all_gm), "shard", scatter_dimension=0, tiled=True
    )
    grad_qkv, grad_out, grad_in, grad_down = (
        lax.psum(row_share[:, : 3 * width].astype(jnp.bfloat16), "rep").astype(jnp.float32),
        lax.psum(row_share[:, 3 * width : 4 * width].astype(jnp.bfloat16), "rep").astype(
            jnp.float32
        ),
        lax.psum(row_share[:, 4 * width :].astype(jnp.bfloat16), "rep").astype(jnp.float32),
        lax.psum(down_share.astype(jnp.bfloat16), "rep").astype(jnp.float32),
    )
    result = jnp.stack(outputs, axis=0)[:, None]
    grad_tokens = jnp.stack(grad_inputs, axis=0)[:, None]
    return (result, grad_tokens, grad_qkv, grad_out, grad_in, grad_down)


def solution(mesh):
    placed = (
        P(None, ("rep", "shard"), None, None),
        P(None, ("rep", "shard")),
        P("shard", None),
        P("shard", None),
        P("shard", None),
        P("shard", None),
        P(None, ("rep", "shard"), None, None),
    )
    return jax.shard_map(
        local,
        mesh=mesh,
        in_specs=placed,
        out_specs=(
            P(None, ("rep", "shard"), None, None),
            P(None, ("rep", "shard"), None, None),
            P("shard", None),
            P("shard", None),
            P("shard", None),
            P("shard", None),
        ),
        check_vma=False,
    )
```

profile of v0, /device:TPU:0, one launch (start us, length us, event | category | flops | bytes accessed | tf_op | source)
XLA Modules:
  0.0 870.6 jit_solution(7404513328902034223)
XLA Ops:
  16.0 1.7 slice_bitcast_fusion.1
  17.9 57.0 %all-gather.5.cloned.1.call-done = bf16[1024,3072]{1,0:T(8,128)(2,1)} async-done(((bf16[64,3072]{1,0:T(8,128)(2,1)}), bf16[1024,3072]{1,0:T(8,128)(2,1)}) %all-gather.5.cloned.1.call-update) | async-done | bytes 6291472 | tf_op jit(solution)/shard_map/all_gather | solution.py:96
  74.9 4.0 fusion.154
  79.6 4.0 fusion.156
  87.9 29.1 %all-gather.7.cloned.1.call-done = bf16[1024,1024]{1,0:T(8,128)(2,1)} async-done(((bf16[64,1024]{1,0:T(8,128)(2,1)}), bf16[1024,1024]{1,0:T(8,128)(2,1)}) %all-gather.7.cloned.1.call-update) | async-done | bytes 2097168 | tf_op jit(solution)/shard_map/all_gather | solution.py:97
  117.0 2.3 fusion.153
  123.6 88.8 %all-gather.9.cloned.1.call-done = bf16[1024,5632]{1,0:T(8,128)(2,1)} async-done(((bf16[64,5632]{1,0:T(8,128)(2,1)}), bf16[1024,5632]{1,0:T(8,128)(2,1)}) %all-gather.9.cloned.1.call-update) | async-done | bytes 11534352 | tf_op jit(solution)/shard_map/all_gather | solution.py:98
  212.4 7.7 fusion.157
  220.2 3.3 fusion.155
  223.5 48.3 %all-gather.11.cloned.1.call-done = bf16[2816,1024]{1,0:T(8,128)(2,1)} async-done(((bf16[176,1024]{1,0:T(8,128)(2,1)}), bf16[2816,1024]{1,0:T(8,128)(2,1)}) %all-gather.11.cloned.1.call-update) | async-done | bytes 5767184 | tf_op jit(solution)/shard_map/all_gather | solution.py:99
  271.8 5.9 multiply_convert_fusion.1
  277.8 2.8 multiply_convert_fusion.3
  281.3 6.1 fusion.46
  289.0 8.9 %fusion.140 = (f32[64]{0:T(128)S(1)}, f32[64]{0:T(128)S(1)}, f32[64,1024]{1,0:T(8,128)S(1)}) fusion(f32[64]{0:T(128)} %copy-done.65, f32[64,1024]{1,0:T(8,128)} %copy-done.3, f32[64]{0:T(128)} %copy-done.57, bf16[1024,5632]{1,0:T(8,128)(2,1)} %all-gather.9.cloned.1.call-done, bf16[64,2816]{1,0:T(8,128)(2,1)} %get-tuple-element.35, ...), kind=kOutput, calls=%fused_computation.237 | convolution fusion | flops 739966848 | bytes 12780544 | tf_op jit(solution)/shard_map/dot_general | solution.py:47
  298.0 9.5 %fusion.139 = (f32[64]{0:T(128)S(1)}, f32[64]{0:T(128)S(1)}, f32[64,1024]{1,0:T(8,128)S(1)}) fusion(f32[64]{0:T(128)S(1)} %copy-done.64, f32[64,1024]{1,0:T(8,128)S(1)} %get-tuple-element.91, f32[64]{0:T(128)S(1)} %copy-done.56, bf16[1024,5632]{1,0:T(8,128)(2,1)} %all-gather.9.cloned.1.call-done, bf16[64,2816]{1,0:T(8,128)(2,1)S(1)} %copy-done.26, ...), kind=kOutput, calls=%fused_computation.236 | convolution fusion | flops 739966848 | bytes 12780544 | tf_op jit(solution)/shard_map/dot_general | solution.py:47
  310.7 1.8 copy.66
  312.5 2.3 convolution_convert_fusion.5
  316.0 1.9 fusion.97
  321.8 6.5 fusion.26
  328.3 10.9 %fusion = f32[1024,5632]{1,0:T(8,128)} fusion(bf16[64,2816]{1,0:T(8,128)(2,1)S(1)} %copy-done.23, bf16[64,2816]{1,0:T(8,128)(2,1)S(1)} %copy-done.22, bf16[64,2816]{1,0:T(8,128)(2,1)S(1)} %copy-done.27, bf16[64,2816]{1,0:T(8,128)(2,1)S(1)} %copy-done.25, bf16[64,1024]{1,0:T(8,128)(2,1)S(1)} %copy-done.16, bf16[64,1024]{1,0:T(8,128)(2,1)S(1)} %fusion.122), kind=kOutput, calls=%fused_computation.1 | convolution fusion | flops 1482686464 | bytes 24772608 | tf_op jit(solution)/shard_map/dot_general | solution.py:53
  339.2 26.3 %pad_maximum_fusion = f32[1024,9728]{1,0:T(8,128)} fusion(f32[1024,5632]{1,0:T(8,128)} %fusion, f32[1024,1024]{1,0:T(8,128)S(1)} %fusion.97, f32[1024,3072]{1,0:T(8,128)} %fusion.26), kind=kLoop, calls=%fused_computation | loop fusion | flops 19922944 | bytes 79691776 | tf_op jit(solution)/shard_map/concatenate | solution.py:179
  366.6 3.9 fusion.12
  370.5 3.9 fusion.13
  375.1 4.8 fusion.20
  380.0 32.5 %reduce-scatter.5.cloned.1.call-done = f32[176,1024]{1,0:T(8,128)} async-done(((f32[2816,1024]{1,0:T(8,128)}), f32[176,1024]{1,0:T(8,128)}) %reduce-scatter.5.cloned.1.call-update) | async-done | bytes 720912 | tf_op jit(solution)/shard_map/reduce_scatter | solution.py:184
  412.5 1.9 convert_element_type.173
  414.4 386.4 %reduce-scatter.3.cloned.1.call-done = f32[64,9728]{1,0:T(8,128)} async-done(((f32[1024,9728]{1,0:T(8,128)}), f32[64,9728]{1,0:T(8,128)}) %reduce-scatter.3.cloned.1.call-update) | async-done | bytes 2490384 | tf_op jit(solution)/shard_map/reduce_scatter | solution.py:178
  800.7 1.8 convert.61
  805.1 5.0 fusion.138
  811.2 45.8 %all-reduce.3.cloned.1.call-done = (bf16[64,3072]{1,0:T(8,128)(2,1)}, bf16[64,1024]{1,0:T(8,128)(2,1)}, bf16[64,5632]{1,0:T(8,128)(2,1)}, bf16[176,1024]{1,0:T(8,128)(2,1)}) async-done(((bf16[64,3072]{1,0:T(8,128)(2,1)}, bf16[64,1024]{1,0:T(8,128)(2,1)}, bf16[64,5632]{1,0:T(8,128)(2,1)}, bf16[176,1024]{1,0:T(8,128)(2,1)}), (bf16[64,3072]{1,0:T(8,128)(2,1)}, bf16[64,1024]{1,0:T(8,128)(2,1)}, ...) | async-done | bytes 1605648 | tf_op jit(solution)/shard_map/psum | solution.py:188
  858.7 1.9 convert_element_type.170
  860.7 1.9 convert_element_type.174
  (228 shorter events, 36.4 us)
Async XLA Ops:
  7.2 10.5 %copy-start.6 = (bf16[2,1,64,1024]{3,2,1,0:T(8,128)(2,1)S(1)}, bf16[2,1,64,1024]{3,2,1,0:T(8,128)(2,1)}, u32[]{:S(2)}) copy-start(bf16[2,1,64,1024]{3,2,1,0:T(8,128)(2,1)} %param.7) | copy-start | bytes 786436
  7.2 67.7 %all-gather.5.cloned.1.call-start = ((), (), s32[]{:S(2)}) async-start(), calls=%async_computation.2 | async-start | bytes 6684672 | tf_op jit(solution)/shard_map/all_gather | solution.py:96
  7.9 109.1 %all-gather.7.cloned.1.call-start = ((), (), s32[]{:S(2)}) async-start(), calls=%async_computation.3 | async-start | bytes 2228224 | tf_op jit(solution)/shard_map/all_gather | solution.py:97
  8.7 203.8 %all-gather.9.cloned.1.call-start = ((), (), s32[]{:S(2)}) async-start(), calls=%async_computation.4 | async-start | bytes 12255232 | tf_op jit(solution)/shard_map/all_gather | solution.py:98
  9.4 262.4 %all-gather.11.cloned.1.call-start = ((), (), s32[]{:S(2)}) async-start(), calls=%async_computation.5 | async-start | bytes 6127616 | tf_op jit(solution)/shard_map/all_gather | solution.py:99
  10.0 402.5 %reduce-scatter.5.cloned.1.call-start = ((), (), s32[]{:S(2)}) async-start(), calls=%async_computation.7 | async-start | bytes 12255232 | tf_op jit(solution)/shard_map/reduce_scatter | solution.py:184
  14.6 60.3 %copy-start.51 = (f32[64]{0:T(128)}, f32[64]{0:T(128)S(1)}, u32[]{:S(2)}) copy-start(f32[64]{0:T(128)S(1)} %get-tuple-element.100) | copy-start | bytes 772
  14.6 60.3 %copy-start.53 = (f32[64]{0:T(128)}, f32[64]{0:T(128)S(1)}, u32[]{:S(2)}) copy-start(f32[64]{0:T(128)S(1)} %get-tuple-element.101) | copy-start | bytes 772
  15.8 59.1 %copy-start.59 = (f32[64]{0:T(128)}, f32[64]{0:T(128)S(1)}, u32[]{:S(2)}) copy-start(f32[64]{0:T(128)S(1)} %add_rsqrt_fusion.3) | copy-start | bytes 772
  15.8 59.1 %copy-start.61 = (f32[64]{0:T(128)}, f32[64]{0:T(128)S(1)}, u32[]{:S(2)}) copy-start(f32[64]{0:T(128)S(1)} %add_rsqrt_fusion.1) | copy-start | bytes 772
  17.9 61.0 %copy-start.28 = (bf16[64,1024]{1,0:T(8,128)(2,1)}, bf16[64,1024]{1,0:T(8,128)(2,1)S(1)}, u32[]{:S(2)}) copy-start(bf16[64,1024]{1,0:T(8,128)(2,1)S(1)} %get-tuple-element.64) | copy-start | bytes 393220
  17.9 61.7 %copy-start.30 = (bf16[64,1024]{1,0:T(8,128)(2,1)}, bf16[64,1024]{1,0:T(8,128)(2,1)S(1)}, u32[]{:S(2)}) copy-start(bf16[64,1024]{1,0:T(8,128)(2,1)S(1)} %get-tuple-element.65) | copy-start | bytes 393220
  79.1 8.5 copy-start.35
  87.6 32.0 %copy-start.49 = (f32[16,64]{1,0:T(8,128)}, f32[16,64]{1,0:T(8,128)S(1)}, u32[]{:S(2)}) copy-start(f32[16,64]{1,0:T(8,128)S(1)} %fusion.64) | copy-start | bytes 12292
  87.9 31.7 %copy-start.33 = (bf16[16,64,64]{2,1,0:T(8,128)(2,1)}, bf16[16,64,64]{2,1,0:T(8,128)(2,1)S(1)}, u32[]{:S(2)}) copy-start(bf16[16,64,64]{2,1,0:T(8,128)(2,1)S(1)} %convolution_convert_fusion.3) | copy-start | bytes 393220
  212.4 7.8 copy-start
  271.8 5.9 copy-start.41
  287.5 513.3 %reduce-scatter.3.cloned.1.call-start = ((), (), s32[]{:S(2)}) async-start(), calls=%async_computation.6 | async-start | bytes 42336256 | tf_op jit(solution)/shard_map/reduce_scatter | solution.py:178
  289.0 9.0 %copy-start.24 = (bf16[64,2816]{1,0:T(8,128)(2,1)S(1)}, bf16[64,2816]{1,0:T(8,128)(2,1)}, u32[]{:S(2)}) copy-start(bf16[64,2816]{1,0:T(8,128)(2,1)} %get-tuple-element.32) | copy-start | bytes 1081348
  289.0 9.0 %copy-start.26 = (bf16[64,2816]{1,0:T(8,128)(2,1)S(1)}, bf16[64,2816]{1,0:T(8,128)(2,1)}, u32[]{:S(2)}) copy-start(bf16[64,2816]{1,0:T(8,128)(2,1)} %get-tuple-element.33) | copy-start | bytes 1081348
  289.0 9.0 %copy-start.56 = (f32[64]{0:T(128)S(1)}, f32[64]{0:T(128)}, u32[]{:S(2)}) copy-start(f32[64]{0:T(128)} %copy-done.55) | copy-start | bytes 772
  289.0 9.0 %copy-start.64 = (f32[64]{0:T(128)S(1)}, f32[64]{0:T(128)}, u32[]{:S(2)}) copy-start(f32[64]{0:T(128)} %copy-done.63) | copy-start | bytes 772
  298.0 9.6 %copy-start.4 = (f32[64,1024]{1,0:T(8,128)S(1)}, f32[64,1024]{1,0:T(8,128)}, u32[]{:S(2)}) copy-start(f32[64,1024]{1,0:T(8,128)} %copy-done.3) | copy-start | bytes 786436
  298.0 9.6 %copy-start.42 = (bf16[2,1,64,1024]{3,2,1,0:T(8,128)(2,1)S(1)}, bf16[2,1,64,1024]{3,2,1,0:T(8,128)(2,1)}, u32[]{:S(2)}) copy-start(bf16[2,1,64,1024]{3,2,1,0:T(8,128)(2,1)} %param.13) | copy-start | bytes 786436
  298.0 9.6 %copy-start.58 = (f32[64]{0:T(128)S(1)}, f32[64]{0:T(128)}, u32[]{:S(2)}) copy-start(f32[64]{0:T(128)} %copy-done.57) | copy-start | bytes 772
  298.0 9.6 %copy-start.66 = (f32[64]{0:T(128)S(1)}, f32[64]{0:T(128)}, u32[]{:S(2)}) copy-start(f32[64]{0:T(128)} %copy-done.65) | copy-start | bytes 772
  321.8 6.5 copy-start.16
  321.8 6.5 copy-start.22
  321.8 6.5 copy-start.23
  321.8 6.5 copy-start.25
  321.8 6.5 copy-start.27
  365.6 491.5 %all-reduce.3.cloned.1.call-start = ((), (), s32[]{:S(2)}) async-start(), calls=%async_computation.8 | async-start | bytes 3211264 | tf_op jit(solution)/shard_map/psum | solution.py:188
  (42 other events, 98.6 us)
Sparse Core Ops, SparseCore 0:
  10.3 64.5 all-gather.4
  77.0 39.9 all-gather.6
  119.3 93.0 all-gather.8
  214.6 57.1 all-gather.10
  287.6 124.8 reduce-scatter.4
  417.3 383.4 reduce-scatter.2
  805.1 51.8 all-reduce.2
where the time goes:
time: 871 us
  waiting for transfers between devices  690 us (79%)
  matrix products  100 us (11%)
  other arithmetic  49.7 us (6%)
  between operations  15.2 us (2%)
  local copies, waits for them, and re-layouts  14.9 us (2%)
    reduce_scatter x1, waiting for transfers between devices, local(): lax.psum_scatter(jnp.concatenate([part_one, part_two, part_three], axis=1...  386 us
    all_gather x1, waiting for transfers between devices, local(): lax.all_gather(in_weight, 'shard', axis=0, tiled=True)  88.8 us
    all_gather x1, waiting for transfers between devices, local(): lax.all_gather(qkv_weight, 'shard', axis=0, tiled=True)  57 us
    all_gather x1, waiting for transfers between devices, local(): lax.all_gather(down_weight, 'shard', axis=0, tiled=True)  48.3 us
    psum x1, waiting for transfers between devices, local(): lax.psum(row_share[:, :3 * width].astype(jnp.bfloat16), 'rep')  45.8 us
    dot_general x8, matrix products, transpose_dot(): lax.dot_general(left, right, (((1,), (1,)), ((), ())), preferred_element_...  40.7 us
    reduce_scatter x1, waiting for transfers between devices, local(): lax.psum_scatter(inner_rows(all_hid, all_gm), 'shard', scatter_dimension=...  32.5 us
    all_gather x1, waiting for transfers between devices, local(): lax.all_gather(out_weight, 'shard', axis=0, tiled=True)  29.1 us
  transfers between devices with their start and end apart: 7, of which 7 were waited for; matrix products, arithmetic and copies ran while one was open for 15% of the time, Pallas kernels for 0%

commit v1 on v0

--- a/solution.py
+++ b/solution.py
@@ -5,6 +5,18 @@
 
 H = 16
 HD = 64
+
+
+def collect(x, axis, dim):
+    ways, here = (lax.axis_size(axis), lax.axis_index(axis))
+    grown, reach = (x, 1)
+    while reach < ways:
+        theirs = lax.ppermute(grown, axis, [(d, d ^ reach) for d in range(ways)])
+        mine_first = jnp.concatenate([grown, theirs], axis=dim)
+        theirs_first = jnp.concatenate([theirs, grown], axis=dim)
+        grown = jnp.where(here & reach == 0, mine_first, theirs_first)
+        reach = 2 * reach
+    return grown
 
 
 def norm_rows(values):
@@ -95,7 +107,7 @@
     full_set = (
         lax.all_gather(qkv_weight, "shard", axis=0, tiled=True),
         lax.all_gather(out_weight, "shard", axis=0, tiled=True),
-        lax.all_gather(in_weight, "shard", axis=0, tiled=True),
+        collect(in_weight, "shard", 0),
         lax.all_gather(down_weight, "shard", axis=0, tiled=True),
     )
     outputs = []

time: 871 us -> 1090 us (1.25)
  waiting for transfers between devices: 690 us -> 877 us
  other arithmetic: 49.7 us -> 72.5 us
    ppermute x0 -> x4, waiting for transfers between devices: none -> 407 us  [collect(): theirs = lax.ppermute(grown, axis, [(d, d ^ reach) for d in range(ways)])]
    all_gather x1 -> x0, waiting for transfers between devices: 88.8 us -> none  [local(): lax.all_gather(in_weight, 'shard', axis=0, tiled=True)]
    all_gather x1, waiting for transfers between devices: 57 us -> 0.02 us  [local(): lax.all_gather(qkv_weight, 'shard', axis=0, tiled=True)]
    all_gather x1, waiting for transfers between devices: 48.3 us -> 0.01 us  [local(): lax.all_gather(down_weight, 'shard', axis=0, tiled=True)]
    all_gather x1, waiting for transfers between devices: 29.1 us -> 0.01 us  [local(): lax.all_gather(out_weight, 'shard', axis=0, tiled=True)]
    select_n x0 -> x4, other arithmetic: none -> 28.3 us  [collect(): grown = jnp.where(here & reach == 0, mine_first, theirs_first)]
  transfers between devices with their start and end apart: 7 -> 10, of which waited for: 7 -> 7; matrix products, arithmetic and copies ran while one was open for 15% -> 14% of each run, Pallas kernels for 0% -> 0%
where the time goes in v1:
time: 1090 us
  waiting for transfers between devices  877 us (80%)
  matrix products  101 us (9%)
  other arithmetic  72.5 us (7%)
  between operations  15.6 us (1%)
  local copies, waits for them, and re-layouts  13.1 us (1%)
    ppermute x4, waiting for transfers between devices, collect(): theirs = lax.ppermute(grown, axis, [(d, d ^ reach) for d in range(ways)])  407 us
    reduce_scatter x1, waiting for transfers between devices, local(): lax.psum_scatter(jnp.concatenate([part_one, part_two, part_three], axis=1...  386 us
    psum x1, waiting for transfers between devices, local(): lax.psum(row_share[:, :3 * width].astype(jnp.bfloat16), 'rep')  45.8 us
    dot_general x8, matrix products, transpose_dot(): lax.dot_general(left, right, (((1,), (1,)), ((), ())), preferred_element_...  40.3 us
    reduce_scatter x1, waiting for transfers between devices, local(): lax.psum_scatter(inner_rows(all_hid, all_gm), 'shard', scatter_dimension=...  38.6 us
    select_n x4, other arithmetic, collect(): grown = jnp.where(here & reach == 0, mine_first, theirs_first)  28.3 us
    dot_general x4, matrix products, inner_rows(): lax.dot_general(left, right, (((0,), (0,)), ((), ())), preferred_element_...  26.4 us
    concatenate x1, other arithmetic, local(): jnp.concatenate([part_one, part_two, part_three], axis=1)  24.9 us
  transfers between devices with their start and end apart: 10, of which 7 were waited for; matrix products, arithmetic and copies ran while one was open for 14% of the time, Pallas kernels for 0%

profile of v1, /device:TPU:0, one launch (start us, length us, event | category | flops | bytes accessed | tf_op | source)
XLA Modules:
  0.0 1087.5 jit_solution(15782246057137677276)
XLA Ops:
  8.5 2.0 collective-permute-done
  12.3 3.0 collective-permute-start.1
  15.2 41.3 %collective-permute-done.1 = bf16[128,5632]{1,0:T(8,128)(2,1)} collective-permute-done((bf16[128,5632]{1,0:T(8,128)(2,1)S(1)}, bf16[128,5632]{1,0:T(8,128)(2,1)}, u32[]{:S(2)}, u32[]{:S(2)}) %collective-permute-start.1) | collective-permute-done | bytes 1441824 | tf_op jit(solution)/shard_map/ppermute | solution.py:14
  56.5 3.0 maximum_select_fusion.2
  61.3 86.4 %collective-permute-done.2 = bf16[256,5632]{1,0:T(8,128)(2,1)} collective-permute-done((bf16[256,5632]{1,0:T(8,128)(2,1)S(1)}, bf16[256,5632]{1,0:T(8,128)(2,1)}, u32[]{:S(2)}, u32[]{:S(2)}) %collective-permute-start.2) | collective-permute-done | bytes 2883616 | tf_op jit(solution)/shard_map/ppermute | solution.py:14
  147.7 6.9 maximum_select_fusion.1
  154.6 2.5 collective-permute-start.3
  161.4 276.8 %collective-permute-done.3 = bf16[512,5632]{1,0:T(8,128)(2,1)} collective-permute-done((bf16[512,5632]{1,0:T(8,128)(2,1)}, bf16[512,5632]{1,0:T(8,128)(2,1)}, u32[]{:S(2)}, u32[]{:S(2)}) %collective-permute-start.3) | collective-permute-done | bytes 5767200 | tf_op jit(solution)/shard_map/ppermute | solution.py:14
  438.2 16.6 %maximum_select_fusion = bf16[1024,5632]{1,0:T(8,128)(2,1)} fusion(bf16[512,5632]{1,0:T(8,128)(2,1)} %collective-permute-done.3, bf16[512,5632]{1,0:T(8,128)(2,1)} %maximum_select_fusion.1, pred[]{:T(512)S(6)} %eq.12), kind=kLoop, calls=%fused_computation.1 | loop fusion | flops 51904512 | bytes 23068672 | tf_op jit(solution)/shard_map/jit(_where)/select_n | solution.py:17
  454.9 4.0 fusion.154
  459.5 4.0 fusion.156
  468.5 2.4 fusion.153
  474.6 7.6 fusion.157
  482.2 3.3 fusion.155
  485.6 5.9 multiply_convert_fusion.1
  491.5 2.8 multiply_convert_fusion.3
  495.1 6.4 fusion.46
  501.6 8.3 fusion.140
  509.9 9.5 fusion.139
  524.5 2.4 convolution_convert_fusion.5
  528.1 1.9 fusion.97
  533.9 7.1 fusion.26
  541.0 11.0 %fusion = f32[1024,5632]{1,0:T(8,128)} fusion(bf16[64,2816]{1,0:T(8,128)(2,1)S(1)} %copy-done.24, bf16[64,2816]{1,0:T(8,128)(2,1)S(1)} %copy-done.23, bf16[64,2816]{1,0:T(8,128)(2,1)S(1)} %copy-done.28, bf16[64,2816]{1,0:T(8,128)(2,1)S(1)} %copy-done.26, bf16[64,1024]{1,0:T(8,128)(2,1)S(1)} %copy-done.17, bf16[64,1024]{1,0:T(8,128)(2,1)S(1)} %fusion.122), kind=kOutput, calls=%fused_computation.5 | convolution fusion | flops 1482686464 | bytes 24772608 | tf_op jit(solution)/shard_map/dot_general | solution.py:65
  552.1 24.9 %pad_maximum_fusion = f32[1024,9728]{1,0:T(8,128)} fusion(f32[1024,5632]{1,0:T(8,128)} %fusion, f32[1024,1024]{1,0:T(8,128)S(1)} %fusion.97, f32[1024,3072]{1,0:T(8,128)} %fusion.26), kind=kLoop, calls=%fused_computation | loop fusion | flops 19922944 | bytes 79691776 | tf_op jit(solution)/shard_map/concatenate | solution.py:191
  578.1 3.7 fusion.12
  581.8 3.8 fusion.13
  586.3 5.0 fusion.20
  591.3 38.6 %reduce-scatter.5.cloned.1.call-done = f32[176,1024]{1,0:T(8,128)} async-done(((f32[2816,1024]{1,0:T(8,128)}), f32[176,1024]{1,0:T(8,128)}) %reduce-scatter.5.cloned.1.call-update) | async-done | bytes 720912 | tf_op jit(solution)/shard_map/reduce_scatter | solution.py:196
  631.8 385.7 %reduce-scatter.3.cloned.1.call-done = f32[64,9728]{1,0:T(8,128)} async-done(((f32[1024,9728]{1,0:T(8,128)}), f32[64,9728]{1,0:T(8,128)}) %reduce-scatter.3.cloned.1.call-update) | async-done | bytes 2490384 | tf_op jit(solution)/shard_map/reduce_scatter | solution.py:190
  1021.8 5.0 fusion.138
  1028.0 45.8 %all-reduce.3.cloned.1.call-done = (bf16[64,3072]{1,0:T(8,128)(2,1)}, bf16[64,1024]{1,0:T(8,128)(2,1)}, bf16[64,5632]{1,0:T(8,128)(2,1)}, bf16[176,1024]{1,0:T(8,128)(2,1)}) async-done(((bf16[64,3072]{1,0:T(8,128)(2,1)}, bf16[64,1024]{1,0:T(8,128)(2,1)}, bf16[64,5632]{1,0:T(8,128)(2,1)}, bf16[176,1024]{1,0:T(8,128)(2,1)}), (bf16[64,3072]{1,0:T(8,128)(2,1)}, bf16[64,1024]{1,0:T(8,128)(2,1)}, ...) | async-done | bytes 1605648 | tf_op jit(solution)/shard_map/psum | solution.py:200
  1075.5 1.9 convert_element_type.170
  (250 shorter events, 42.4 us)
Async XLA Ops:
  7.2 447.7 %all-gather.4.cloned.1.call-start = ((), (), s32[]{:S(2)}) async-start(), calls=%async_computation.2 | async-start | bytes 6684672 | tf_op jit(solution)/shard_map/all_gather | solution.py:108
  7.9 460.6 %all-gather.6.cloned.1.call-start = ((), (), s32[]{:S(2)}) async-start(), calls=%async_computation.3 | async-start | bytes 2228224 | tf_op jit(solution)/shard_map/all_gather | solution.py:109
  7.9 2.5 collective-permute-start
  12.3 44.3 %collective-permute-start.1 = (bf16[128,5632]{1,0:T(8,128)(2,1)S(1)}, bf16[128,5632]{1,0:T(8,128)(2,1)}, u32[]{:S(2)}, u32[]{:S(2)}) collective-permute-start(bf16[128,5632]{1,0:T(8,128)(2,1)S(1)} %maximum_select_fusion.3), channel_id=1, source_target_pairs={{0,2},{1,3},{2,0},{3,1},{4,6},{5,7},{6,4},{7,5},{8,10},{9,11},{10,... | collective-permute-start | bytes 4325384 | tf_op jit(solution)/shard_map/ppermute | solution.py:14
  59.6 88.1 %collective-permute-start.2 = (bf16[256,5632]{1,0:T(8,128)(2,1)S(1)}, bf16[256,5632]{1,0:T(8,128)(2,1)}, u32[]{:S(2)}, u32[]{:S(2)}) collective-permute-start(bf16[256,5632]{1,0:T(8,128)(2,1)S(1)} %maximum_select_fusion.2), channel_id=1, source_target_pairs={{0,4},{1,5},{2,6},{3,7},{4,0},{5,1},{6,2},{7,3},{8,12},{9,13},{10,... | collective-permute-start | bytes 8650760 | tf_op jit(solution)/shard_map/ppermute | solution.py:14
  61.2 424.4 %all-gather.8.cloned.1.call-start = ((), (), s32[]{:S(2)}) async-start(), calls=%async_computation.4 | async-start | bytes 6127616 | tf_op jit(solution)/shard_map/all_gather | solution.py:111
  61.2 96.0 %copy-start.69 = (s32[2,1]{0,1:T(1,128)S(1)}, s32[2,1]{0,1:T(1,128)}, u32[]{:S(2)}) copy-start(s32[2,1]{0,1:T(1,128)} %param.8) | copy-start | bytes 28
  61.2 98.6 %copy-start.5 = (bf16[2,1,64,1024]{3,2,1,0:T(8,128)(2,1)S(1)}, bf16[2,1,64,1024]{3,2,1,0:T(8,128)(2,1)}, u32[]{:S(2)}) copy-start(bf16[2,1,64,1024]{3,2,1,0:T(8,128)(2,1)} %param.7) | copy-start | bytes 786436
  61.3 99.2 %copy-start.41 = (bf16[2,1,64,1024]{3,2,1,0:T(8,128)(2,1)S(1)}, bf16[2,1,64,1024]{3,2,1,0:T(8,128)(2,1)}, u32[]{:S(2)}) copy-start(bf16[2,1,64,1024]{3,2,1,0:T(8,128)(2,1)} %param.13) | copy-start | bytes 786436
  154.6 283.6 %collective-permute-start.3 = (bf16[512,5632]{1,0:T(8,128)(2,1)}, bf16[512,5632]{1,0:T(8,128)(2,1)}, u32[]{:S(2)}, u32[]{:S(2)}) collective-permute-start(bf16[512,5632]{1,0:T(8,128)(2,1)} %maximum_select_fusion.1), channel_id=1, source_target_pairs={{0,8},{1,9},{2,10},{3,11},{4,12},{5,13},{6,14},{7,15},{8,0},{9,1},... | collective-permute-start | bytes 17301512 | tf_op jit(solution)/shard_map/ppermute | solution.py:14
  157.1 472.8 %reduce-scatter.5.cloned.1.call-start = ((), (), s32[]{:S(2)}) async-start(), calls=%async_computation.6 | async-start | bytes 12255232 | tf_op jit(solution)/shard_map/reduce_scatter | solution.py:196
  160.0 294.8 %copy-start.53 = (f32[64]{0:T(128)}, f32[64]{0:T(128)S(1)}, u32[]{:S(2)}) copy-start(f32[64]{0:T(128)S(1)} %get-tuple-element.100) | copy-start | bytes 772
  160.0 294.8 %copy-start.55 = (f32[64]{0:T(128)}, f32[64]{0:T(128)S(1)}, u32[]{:S(2)}) copy-start(f32[64]{0:T(128)S(1)} %get-tuple-element.101) | copy-start | bytes 772
  160.3 294.5 %copy-start.61 = (f32[64]{0:T(128)}, f32[64]{0:T(128)S(1)}, u32[]{:S(2)}) copy-start(f32[64]{0:T(128)S(1)} %add_rsqrt_fusion.3) | copy-start | bytes 772
  160.3 294.5 %copy-start.63 = (f32[64]{0:T(128)}, f32[64]{0:T(128)S(1)}, u32[]{:S(2)}) copy-start(f32[64]{0:T(128)S(1)} %add_rsqrt_fusion.1) | copy-start | bytes 772
  161.4 293.4 %copy-start.29 = (bf16[64,1024]{1,0:T(8,128)(2,1)}, bf16[64,1024]{1,0:T(8,128)(2,1)S(1)}, u32[]{:S(2)}) copy-start(bf16[64,1024]{1,0:T(8,128)(2,1)S(1)} %get-tuple-element.64) | copy-start | bytes 393220
  161.4 298.1 %copy-start.31 = (bf16[64,1024]{1,0:T(8,128)(2,1)}, bf16[64,1024]{1,0:T(8,128)(2,1)S(1)}, u32[]{:S(2)}) copy-start(bf16[64,1024]{1,0:T(8,128)(2,1)S(1)} %get-tuple-element.65) | copy-start | bytes 393220
  459.1 8.4 copy-start.35
  473.0 9.2 slice-start
  474.6 7.7 copy-start.16
  474.6 7.7 slice-start.1
  474.6 7.7 slice-start.2
  501.5 516.0 %reduce-scatter.3.cloned.1.call-start = ((), (), s32[]{:S(2)}) async-start(), calls=%async_computation.5 | async-start | bytes 42336256 | tf_op jit(solution)/shard_map/reduce_scatter | solution.py:190
  501.5 8.3 copy-start.25
  501.6 8.3 copy-start.27
  501.6 8.3 copy-start.58
  501.6 8.3 copy-start.66
  509.9 9.6 copy-start.3
  509.9 9.6 copy-start.43
  509.9 9.6 copy-start.60
  509.9 9.6 copy-start.68
  577.0 496.7 %all-reduce.3.cloned.1.call-start = ((), (), s32[]{:S(2)}) async-start(), calls=%async_computation.7 | async-start | bytes 3211264 | tf_op jit(solution)/shard_map/psum | solution.py:200
  (51 other events, 156.8 us)
Sparse Core Ops, SparseCore 0:
  10.3 76.1 all-gather.3
  88.6 50.2 all-gather.5
  157.2 187.3 all-gather.7
  501.6 128.2 reduce-scatter.4
  634.6 382.7 reduce-scatter.2
  1021.8 51.8 all-reduce.2
